TPU v7x, 32 devices: a whole 2x2x4 slice. The times are simulated.
32 devices in a mesh: leaf: 4 (over z), bits: 8 (over y, x, core).
Axes of the slice: x: 2, y: 2, z: 4, core: 2. Of those that a mesh axis runs over, the one named last changes fastest.
Arguments:
- state: float32 [2, 4, 8, 4096, 256], P(None, 'leaf', 'bits'), may hold values from -6 to 6
- gate_one: float32 [2, 512, 512], replicated, may hold values from -0.1875 to 0.1875
- gate_two: float32 [2, 512, 512], replicated, may hold values from -0.1875 to 0.1875
- row_order: int32 [4096], replicated, may hold values from 0 to 4095, each once
- picks: int32 [8, 4096], P('bits'), may hold values from 0 to 4095, each once within a row
- counts: int32 [8, 4096], P('bits'), may hold values from 1 to 256, as said below
Outputs:
- amplitudes: float32 [2, 8, 4096, 256], P(None, 'bits', 'leaf')
Inputs may be any that keep to these rules, and one draw needn't show every extreme that they name: `counts`: live columns of each block; the first block of every group holds 256. `picks`: each group's blocks name every row once.
All inputs are finite; a program needn't handle non-finite values.
Results may differ from a plain program's by a relative error of at most 0.0001.
Values sent between devices are 32-bit elements; how exact they have to be, the bound alone decides.
A program may use at most 128 MiB of HBM per device.

v0:
```python
import jax
import jax.numpy as jnp
from jax import lax
from jax.sharding import PartitionSpec as P

SWAP_ONE = 0
SWAP_TWO = 2


def from_partner(x, axis, apart):
    return lax.ppermute(x, axis, [(i, i ^ 1 << apart) for i in range(lax.axis_size(axis))])


def complex_product(values, weights):
    stacked = jnp.concatenate([values[0], values[1]], axis=1)
    blocked = jnp.concatenate(
        [
            jnp.concatenate([weights[0], weights[1]], axis=1),
            jnp.concatenate([-weights[1], weights[0]], axis=1),
        ],
        axis=0,
    )
    joined = jnp.dot(
        stacked, blocked, precision=lax.Precision.HIGHEST, preferred_element_type=jnp.float32
    )
    split_at = weights.shape[2]
    return jnp.stack([joined[:, :split_at], joined[:, split_at:]])


def quarter(gate, row_half, col_half, columns):
    return lax.dynamic_slice(
        gate, (0, row_half * columns, col_half * columns), (2, columns, columns)
    )


def shards(state, gate_one, gate_two, row_order, picks, counts):
    columns = state.shape[-1]
    mine_block = state[:, 0, 0]
    group_index = lax.axis_index("bits")
    high_one = group_index >> SWAP_ONE & 1
    high_two = group_index >> SWAP_TWO & 1
    own_term = complex_product(mine_block, quarter(gate_one, high_one, high_one, columns))
    partner = from_partner(mine_block, "bits", SWAP_ONE)
    section_one = own_term + complex_product(
        partner, quarter(gate_one, 1 - high_one, high_one, columns)
    )
    wanted = jnp.take(row_order, picks[0], axis=0)
    own_rows = jnp.take(section_one, wanted, axis=1)
    partner_two = from_partner(section_one, "bits", SWAP_TWO)
    other_rows = jnp.take(partner_two, wanted, axis=1)
    weight_own = quarter(gate_two, high_two, high_two, columns)
    weight_other = quarter(gate_two, 1 - high_two, high_two, columns)
    share_rows = picks.shape[1] // lax.axis_size("leaf")
    amplitude = complex_product(own_rows, weight_own) + complex_product(other_rows, weight_other)
    summed = lax.psum_scatter(amplitude, "leaf", scatter_dimension=1, tiled=True)
    live_counts = lax.dynamic_slice_in_dim(
        counts[0], lax.axis_index("leaf") * share_rows, share_rows
    )
    keep_mask = jnp.arange(columns, dtype=jnp.int32)[None, :] < live_counts[:, None]
    masked = jnp.where(keep_mask[None], summed, jnp.zeros_like(summed))
    return masked[:, None]


def solution(mesh):
    return jax.shard_map(
        shards,
        mesh=mesh,
        in_specs=(
            P(None, "leaf", "bits", None, None),
            P(),
            P(),
            P(),
            P("bits", None),
            P("bits", None),
        ),
        out_specs=P(None, "bits", "leaf", None),
        check_vma=False,
    )
```

profile of v0, /device:TPU:0, one launch (start us, length us, event | category | flops | bytes accessed | tf_op | source)
XLA Modules:
  0.0 542.7 jit_solution(6343499808911651598)
XLA Ops:
  6.5 0.5 collective-permute-start
  7.0 1.1 dynamic-slice_bitcast_fusion.5
  8.1 1.1 fusion.50
  9.2 4.0 slice_bitcast_fusion.11
  13.2 15.8 %fusion = f32[4096,512]{1,0:T(8,128)S(1)} fusion(f32[4096,256]{1,0:T(8,128)S(1)} %get-tuple-element.29, f32[4096,256]{1,0:T(8,128)S(1)} %get-tuple-element.28, f32[256,256]{1,0:T(8,128)S(1)} %get-tuple-element.37, f32[256,256]{1,0:T(8,128)S(1)} %get-tuple-element.34, f32[256,256]{1,0:T(8,128)S(1)} %get-tuple-element.35), kind=kOutput, calls=%fused_computation.3 | convolution fusion | flops 12887785472 | bytes 17563648 | tf_op jit(solution)/shard_map/dot_general | solution.py:23
  29.0 6.0 %slice_bitcast_fusion.7 = (f32[4096,256]{1,0:T(8,128)S(1)}, f32[4096,256]{1,0:T(8,128)}) fusion(f32[2,4096,256]{2,1,0:T(8,128)} %collective-permute-done), kind=kLoop, calls=%fused_computation.30 | loop fusion | bytes 16777216 | tf_op jit(solution)/shard_map/squeeze | solution.py:15
  35.0 16.1 %fusion.4 = f32[4096,512]{1,0:T(8,128)S(1)} fusion(f32[4096,256]{1,0:T(8,128)} %get-tuple-element.25, f32[4096,256]{1,0:T(8,128)S(1)} %get-tuple-element.24, f32[256,256]{1,0:T(8,128)S(1)} %get-tuple-element.36, f32[256,256]{1,0:T(8,128)S(1)} %get-tuple-element.10, f32[256,256]{1,0:T(8,128)S(1)} %get-tuple-element.11), kind=kOutput, calls=%fused_computation.8 | convolution fusion | flops 12887785472 | bytes 17563648 | tf_op jit(solution)/shard_map/dot_general | solution.py:23
  51.1 4.9 slice_bitcast_fusion.5
  56.0 7.8 %maximum_add_fusion = f32[2,4096,256]{2,1,0:T(8,128)} fusion(f32[1,4096,256]{2,1,0:T(8,128)} %get-tuple-element.40, f32[1,4096,256]{2,1,0:T(8,128)} %get-tuple-element.41, f32[1,4096,256]{2,1,0:T(8,128)} %get-tuple-element.23, f32[1,4096,256]{2,1,0:T(8,128)S(1)} %get-tuple-element.22), kind=kLoop, calls=%fused_computation.7 | loop fusion | flops 6291456 | bytes 25165824 | tf_op jit(solution)/shard_map/add | solution.py:44
  63.8 2.5 collective-permute-start.1
  66.4 23.0 %gather_fusion = s32[4096]{0:T(1024)S(1)} fusion(s32[4096]{0:T(1024)S(1)} %copy-done, s32[4096]{0:T(1024)S(1)} %broadcast_clamp_fusion.1), kind=kCustom, calls=%fused_computation.2 | custom fusion | bytes 49152 | tf_op jit(solution)/shard_map/jit(_take)/gather | solution.py:47
  89.4 1.1 dynamic-slice_bitcast_fusion.1
  90.5 1.1 fusion.48
  91.7 15.4 %copy.8 = f32[2,4096,256]{2,0,1:T(2,128)} copy(f32[2,4096,256]{2,1,0:T(8,128)} %maximum_add_fusion) | data formatting | bytes 16777216 | tf_op jit(solution)/shard_map/add | solution.py:44
  107.1 37.5 %gather_fusion.1 = f32[4096,2,256]{2,1,0:T(2,128)} fusion(f32[2,4096,256]{2,0,1:T(2,128)} %copy.8, s32[4096]{0:T(1024)S(1)} %broadcast_clamp_fusion), kind=kCustom, calls=%fused_computation.clone | custom fusion | bytes 16793600 | tf_op jit(solution)/shard_map/jit(_take)/gather | solution.py:48
  144.5 103.2 %collective-permute-done.1 = f32[2,4096,256]{2,1,0:T(8,128)} collective-permute-done((f32[2,4096,256]{2,1,0:T(8,128)}, f32[2,4096,256]{2,1,0:T(8,128)}, u32[]{:S(2)}, u32[]{:S(2)}) %collective-permute-start.1) | collective-permute-done | bytes 8388640 | tf_op jit(solution)/shard_map/ppermute | solution.py:11
  247.8 26.3 %copy.10 = f32[2,4096,256]{2,0,1:T(2,128)} copy(f32[2,4096,256]{2,1,0:T(8,128)} %collective-permute-done.1) | data formatting | bytes 16777216 | tf_op jit(solution)/shard_map/ppermute | solution.py:11
  274.1 37.5 %gather_fusion.2 = f32[4096,2,256]{2,1,0:T(2,128)} fusion(f32[2,4096,256]{2,0,1:T(2,128)} %copy.10, s32[4096]{0:T(1024)S(1)} %broadcast_clamp_fusion), kind=kCustom, calls=%fused_computation.1.clone | custom fusion | bytes 16793600 | tf_op jit(solution)/shard_map/jit(_take)/gather | solution.py:50
  311.6 16.9 %select_bitcast_fusion = (f32[2,4096,256]{2,0,1:T(2,128)S(1)}, f32[2,4096,256]{2,0,1:T(2,128)S(1)}) fusion(f32[4096,2,256]{2,1,0:T(2,128)} %gather_fusion.2, pred[4096]{0:T(1024)(128)(4,1)S(1)} %compare_and_fusion, f32[4096,2,256]{2,1,0:T(2,128)} %gather_fusion.1), kind=kLoop, calls=%fused_computation.21 | loop fusion | flops 4194304 | bytes 33558528 | tf_op jit(solution)/shard_map/jit(_take)/select_n | solution.py:50
  328.5 6.6 %fusion.52 = (f32[1,4096,256]{2,0,1:T(1,128)S(1)}, f32[1,4096,256]{2,0,1:T(1,128)S(1)}) fusion(f32[2,4096,256]{2,0,1:T(2,128)S(1)} %get-tuple-element.38), kind=kLoop, calls=%fused_computation.92 | loop fusion | bytes 16777216 | tf_op jit(solution)/shard_map/slice | solution.py:15
  335.2 0.3 copy.21
  335.4 0.3 copy.23
  335.7 15.8 %fusion.12 = f32[4096,512]{1,0:T(8,128)S(1)} fusion(f32[4096,256]{1,0:T(8,128)S(1)} %bitcast.73, f32[4096,256]{1,0:T(8,128)S(1)} %bitcast.71, f32[256,256]{1,0:T(8,128)S(1)} %get-tuple-element.32, f32[256,256]{1,0:T(8,128)S(1)} %get-tuple-element.6, f32[256,256]{1,0:T(8,128)S(1)} %get-tuple-element.7), kind=kOutput, calls=%fused_computation.17 | convolution fusion | flops 12887785472 | bytes 17563648 | tf_op jit(solution)/shard_map/dot_general | solution.py:23
  351.5 2.5 slice_bitcast_fusion.1
  354.0 6.6 %fusion.53 = (f32[1,4096,256]{2,0,1:T(1,128)S(1)}, f32[1,4096,256]{2,0,1:T(1,128)S(1)}) fusion(f32[2,4096,256]{2,0,1:T(2,128)S(1)} %get-tuple-element.39), kind=kLoop, calls=%fused_computation.93 | loop fusion | bytes 16777216 | tf_op jit(solution)/shard_map/slice | solution.py:15
  361.1 15.8 %fusion.8 = f32[4096,512]{1,0:T(8,128)S(1)} fusion(f32[4096,256]{1,0:T(8,128)S(1)} %bitcast.72, f32[4096,256]{1,0:T(8,128)S(1)} %bitcast.70, f32[256,256]{1,0:T(8,128)S(1)} %get-tuple-element.33, f32[256,256]{1,0:T(8,128)S(1)} %get-tuple-element.30, f32[256,256]{1,0:T(8,128)S(1)} %get-tuple-element.31), kind=kOutput, calls=%fused_computation.12 | convolution fusion | flops 12887785472 | bytes 17563648 | tf_op jit(solution)/shard_map/dot_general | solution.py:23
  376.9 2.7 slice_bitcast_fusion.3
  379.6 1.0 copy-done.2
  380.6 5.4 maximum_add_fusion.1
  386.0 0.7 constant_dynamic-slice_fusion
  386.9 145.3 %reduce-scatter.2.cloned.1.call-done = f32[2,1024,256]{2,1,0:T(8,128)} async-done(((f32[2,4096,256]{2,1,0:T(8,128)}), f32[2,1024,256]{2,1,0:T(8,128)}) %reduce-scatter.2.cloned.1.call-update) | async-done | bytes 2097168 | tf_op jit(solution)/shard_map/reduce_scatter | solution.py:55
  532.3 3.1 select_bitcast_fusion.2
  (17 shorter events, 0.8 us)
Async XLA Ops:
  6.5 59.8 %copy-start = (s32[4096]{0:T(1024)S(1)}, s32[4096]{0:T(1024)}, u32[]{:S(2)}) copy-start(s32[4096]{0:T(1024)} %param.11) | copy-start | bytes 49156
  6.5 525.7 %reduce-scatter.2.cloned.1.call-start = ((), (), s32[]{:S(2)}) async-start(), calls=%async_computation.1 | async-start | bytes 10485760 | tf_op jit(solution)/shard_map/reduce_scatter | solution.py:55
  6.5 22.5 %collective-permute-start = (f32[2,4096,256]{2,1,0:T(8,128)}, f32[2,4096,256]{2,1,0:T(8,128)}, u32[]{:S(2)}, u32[]{:S(2)}) collective-permute-start(f32[2,4096,256]{2,1,0:T(8,128)} %bitcast.74), channel_id=1, source_target_pairs={{0,1},{1,0},{2,3},{3,2},{4,5},{5,4},{6,7},{7,6},{8,9},{9,8},{10,11... | collective-permute-start | bytes 25165832 | tf_op jit(solution)/shard_map/ppermute | solution.py:11
  56.0 10.3 %copy-start.3 = (s32[1,4096]{1,0:T(1,128)S(1)}, s32[1,4096]{1,0:T(1,128)}, u32[]{:S(2)}) copy-start(s32[1,4096]{1,0:T(1,128)} %param.12) | copy-start | bytes 49156
  63.8 183.9 %collective-permute-start.1 = (f32[2,4096,256]{2,1,0:T(8,128)}, f32[2,4096,256]{2,1,0:T(8,128)}, u32[]{:S(2)}, u32[]{:S(2)}) collective-permute-start(f32[2,4096,256]{2,1,0:T(8,128)} %maximum_add_fusion), channel_id=1, source_target_pairs={{0,4},{1,5},{2,6},{3,7},{4,0},{5,1},{6,2},{7,3},{8,12},{9,13},{10,... | collective-permute-start | bytes 25165832 | tf_op jit(solution)/shard_map/ppermute | solution.py:11
  376.9 3.7 copy-start.2
  386.0 149.4 %copy-start.1 = (s32[4096]{0:T(1024)S(1)}, s32[4096]{0:T(1024)}, u32[]{:S(2)}) copy-start(s32[4096]{0:T(1024)} %param.11) | copy-start | bytes 49156
Sparse Core Ops, SparseCore 0:
  386.1 146.0 reduce-scatter.1
where the time goes:
time: 552 us; the launch traced here: 543 us
  waiting for transfers between devices  249 us (45%)
  local copies, waits for them, and re-layouts  178 us (32%)
  matrix products  63.4 us (11%)
  other arithmetic  35.7 us (6%)
  between operations  14 us (3%)
    reduce_scatter x1, waiting for transfers between devices, shards(): lax.psum_scatter(amplitude, 'leaf', scatter_dimension=1, tiled=True)  145 us
    ppermute x2, waiting for transfers between devices, from_partner(): lax.ppermute(x, axis, [(i, i ^ 1 << apart) for i in range(lax.axis_size(a...  103 us
    dot_general x4, matrix products, complex_product(): jnp.dot(stacked, blocked, precision=lax.Precision.HIGHEST, preferred_elem...  63.4 us
    gather x1, local copies, waits for them, and re-layouts, shards(): other_rows = jnp.take(partner_two, wanted, axis=1)  37.5 us
    gather x1, local copies, waits for them, and re-layouts, shards(): own_rows = jnp.take(section_one, wanted, axis=1)  37.5 us
    ppermute x1, local copies, waits for them, and re-layouts, from_partner(): lax.ppermute(x, axis, [(i, i ^ 1 << apart) for i in range(lax.axis_size(a...  26.3 us
    gather x1, local copies, waits for them, and re-layouts, shards(): wanted = jnp.take(row_order, picks[0], axis=0)  23 us
    select_n x1, other arithmetic, shards(): other_rows = jnp.take(partner_two, wanted, axis=1)  16.9 us
  transfers between devices with their start and end apart: 3, of which 2 were waited for; matrix products, arithmetic and copies ran while one was open for 19% of the time, Pallas kernels for 0%

commit v1 on v0

v1 whole, which is shorter than its diff:
```python
import functools

import jax
import jax.numpy as jnp
from jax import lax
from jax.experimental import pallas as pl
from jax.experimental.pallas import tpu as pltpu
from jax.sharding import PartitionSpec as P

SWAP_ONE = 0
SWAP_TWO = 2
GROUPS = 2
PER_GROUP = 2
MESH = pl.DeviceIdType.MESH


def split(x):
    hi = x.astype(jnp.bfloat16)
    lo = (x - hi.astype(jnp.float32)).astype(jnp.bfloat16)
    return hi, lo


def kernel(
    n_leaf, picks_ref, order_ref, state_ref, one_ref, two_ref, out_ref,
    st, rs, ssum, core, sec, ybuf, parts, quarters, w_hi, w_lo,
    local_sem, rs_send, rs_recv, core_send, core_recv, y_send, y_recv, ag_send, ag_recv,
):
    me = lax.axis_index("leaf")
    group = lax.axis_index("bits")
    columns = state_ref.shape[2]
    block = state_ref.shape[1] // n_leaf
    chunks = GROUPS * PER_GROUP
    tall = block // chunks
    rc = tall // 2
    steps = n_leaf - 1
    high_one = group // 2**SWAP_ONE % 2
    high_two = group // 2**SWAP_TWO % 2
    partner_one = group + 2**SWAP_ONE * (1 - 2 * high_one)
    partner_two = group + 2**SWAP_TWO * (1 - 2 * high_two)
    neighbour = [lax.rem(me + 1, n_leaf), lax.rem(me + n_leaf - 1, n_leaf)]

    barrier = pltpu.get_barrier_semaphore()
    for where in (
        {"leaf": neighbour[0]}, {"leaf": neighbour[1]}, {"bits": partner_one}, {"bits": partner_two},
    ):
        pl.semaphore_signal(barrier, inc=1, device_id=where, device_id_type=MESH)
    load = pltpu.make_async_copy(state_ref, st, local_sem.at[0])
    load.start()
    loads = []
    for gate, ref, high in ((0, one_ref, high_one), (1, two_ref, high_two)):
        for other in range(2):
            row_half = high if other == 0 else 1 - high
            loads.append(
                pltpu.make_async_copy(
                    ref.at[:, pl.ds(pl.multiple_of(row_half * columns, columns), columns),
                           pl.ds(pl.multiple_of(high * columns, columns), columns)],
                    quarters.at[gate, other],
                    local_sem.at[1 + 2 * gate + other],
                )
            )
            loads[-1].start()
    pl.semaphore_wait(barrier, 4)

    def rows_of(b, c, d):
        b = lax.rem(b + 2 * n_leaf, n_leaf)
        return pl.ds(pl.multiple_of(b * block + c * tall + d * rc, rc), rc)

    def away(d, k):
        return me - k if d == 0 else me + k

    def rs_copy(d, s, c):
        if isinstance(s, int) and s == 0:
            src = state_ref.at[:, rows_of(away(d, 1), c, d), :]
        else:
            src = rs.at[d, s - 1, c]
        return pltpu.make_async_remote_copy(
            src_ref=src, dst_ref=rs.at[d, s, c],
            send_sem=rs_send.at[d, s, c], recv_sem=rs_recv.at[d, s, c],
            device_id={"leaf": neighbour[d]}, device_id_type=MESH,
        )

    def rs_arrival(d, s, c):
        piece = rs.at[d, s, c]
        return pltpu.make_async_remote_copy(
            src_ref=piece, dst_ref=piece,
            send_sem=rs_send.at[d, s, c], recv_sem=rs_recv.at[d, s, c],
            device_id={"leaf": neighbour[d]}, device_id_type=MESH,
        )

    def core_copy(c):
        return pltpu.make_async_remote_copy(
            src_ref=ssum.at[c], dst_ref=core.at[c],
            send_sem=core_send.at[c], recv_sem=core_recv.at[c],
            device_id={"bits": partner_one}, device_id_type=MESH,
        )

    def y_copy(c):
        return pltpu.make_async_remote_copy(
            src_ref=sec.at[c], dst_ref=ybuf.at[c],
            send_sem=y_send.at[c], recv_sem=y_recv.at[c],
            device_id={"bits": partner_two}, device_id_type=MESH,
        )

    def ag_copy(d, t, c):
        piece = parts.at[:, rows_of(away(d, t), c, d), :]
        return pltpu.make_async_remote_copy(
            src_ref=piece, dst_ref=piece,
            send_sem=ag_send.at[d, t, c], recv_sem=ag_recv.at[d, t, c],
            device_id={"leaf": neighbour[d]}, device_id_type=MESH,
        )

    def ag_arrival(d, t, c):
        piece = parts.at[:, rows_of(away(d, t + 1), c, d), :]
        return pltpu.make_async_remote_copy(
            src_ref=piece, dst_ref=piece,
            send_sem=ag_send.at[d, t, c], recv_sem=ag_recv.at[d, t, c],
            device_id={"leaf": neighbour[d]}, device_id_type=MESH,
        )

    def each(count, body):
        def step(i, carry):
            body(i)
            return carry

        lax.fori_loop(0, count, step, 0)

    def product(gate, mine, theirs):
        x = jnp.concatenate([mine[0], mine[1], theirs[0], theirs[1]], axis=1)
        x_hi, x_lo = split(x)
        dot = functools.partial(jnp.dot, preferred_element_type=jnp.float32)
        return dot(x_hi, w_hi[gate]) + (dot(x_lo, w_hi[gate]) + dot(x_hi, w_lo[gate]))

    def begin(g):
        for k in range(PER_GROUP):
            for d in range(2):
                rs_copy(d, 0, g * PER_GROUP + k).start()

    begin(0)

    for one in loads:
        one.wait()
    for gate in range(2):
        for other in range(2):
            re_hi, re_lo = split(quarters[gate, other, 0])
            im_hi, im_lo = split(quarters[gate, other, 1])
            top = pl.ds(2 * other * columns, columns)
            low = pl.ds((2 * other + 1) * columns, columns)
            left, right = pl.ds(0, columns), pl.ds(columns, columns)
            for w, re, im in ((w_hi, re_hi, im_hi), (w_lo, re_lo, im_lo)):
                w[gate, top, left] = re
                w[gate, top, right] = im
                w[gate, low, left] = -im
                w[gate, low, right] = re
    load.wait()

    def iteration(g):
        first = g * PER_GROUP

        @pl.when(g < GROUPS)
        def _():
            def forward(i):
                s, c = i // PER_GROUP, first + i % PER_GROUP
                for d in range(2):
                    rs_arrival(d, s, c).wait_recv()
                    rs[d, s, c] = rs[d, s, c] + st[:, rows_of(away(d, s + 2), c, d), :]
                    rs_copy(d, s + 1, c).start()

            each((steps - 1) * PER_GROUP, forward)

        @pl.when(g + 1 < GROUPS)
        def _():
            begin(g + 1)

        @pl.when((g >= 2) & (g < GROUPS + 2))
        def _():
            def forward(i):
                t, c = i // PER_GROUP, first - 2 * PER_GROUP + i % PER_GROUP
                for d in range(2):
                    ag_arrival(d, t, c).wait_recv()
                    ag_copy(d, t + 1, c).start()

            each((steps - 1) * PER_GROUP, forward)

        @pl.when((g >= 1) & (g < GROUPS + 1))
        def _():
            def second(k):
                c = first - PER_GROUP + k
                y_copy(c).wait_recv()
                part = product(1, sec[c], ybuf[c])
                here = pl.ds(pl.multiple_of(me * block + c * tall, tall), tall)
                parts[0, here, :] = part[:, :columns]
                parts[1, here, :] = part[:, columns:]
                for d in range(2):
                    ag_copy(d, 0, c).start()

            each(PER_GROUP, second)

        @pl.when(g < GROUPS)
        def _():
            def last(k):
                c = first + k
                for d in range(2):
                    rs_arrival(d, steps - 1, c).wait_recv()
                    ssum[c, :, pl.ds(d * rc, rc), :] = rs[d, steps - 1, c] + st[:, rows_of(me, c, d), :]
                core_copy(c).start()

            def first_step(k):
                c = first + k
                core_copy(c).wait_recv()
                section = product(0, ssum[c], core[c])
                sec[c, 0] = section[:, :columns]
                sec[c, 1] = section[:, columns:]
                y_copy(c).start()

            each(PER_GROUP, last)
            each(PER_GROUP, first_step)

    each(GROUPS + 2, iteration)

    def arrive(c):
        for d in range(2):
            ag_arrival(d, steps - 1, c).wait_recv()

    each(chunks, arrive)

    base = me * block
    unroll = 16

    def pick(i):
        for k in range(unroll):
            p = i * unroll + k
            row = order_ref[picks_ref[0, base + p]]
            out_ref[:, pl.ds(p, 1), :] = parts[:, pl.ds(row, 1), :]

    each(block // unroll, pick)

    def drain(c):
        for d in range(2):
            for s in range(steps):
                rs_copy(d, s, c).wait_send()
                ag_copy(d, s, c).wait_send()
        core_copy(c).wait_send()
        y_copy(c).wait_send()

    each(chunks, drain)


def shards(state, gate_one, gate_two, row_order, picks, counts):
    rows, columns = state.shape[-2:]
    n_leaf = lax.axis_size("leaf")
    block = rows // n_leaf
    chunks = GROUPS * PER_GROUP
    tall = block // chunks
    rc = tall // 2
    steps = n_leaf - 1
    f32, dma = jnp.float32, pltpu.SemaphoreType.DMA
    vmem, smem, hbm = (
        pl.BlockSpec(memory_space=m) for m in (pltpu.VMEM, pltpu.SMEM, pl.ANY)
    )
    picked = pl.pallas_call(
        functools.partial(kernel, n_leaf),
        out_shape=jax.ShapeDtypeStruct((2, block, columns), f32),
        in_specs=[smem, smem, hbm, hbm, hbm],
        out_specs=vmem,
        scratch_shapes=[
            pltpu.VMEM((2, rows, columns), f32),
            pltpu.VMEM((2, steps, chunks, 2, rc, columns), f32),
            pltpu.VMEM((chunks, 2, tall, columns), f32),
            pltpu.VMEM((chunks, 2, tall, columns), f32),
            pltpu.VMEM((chunks, 2, tall, columns), f32),
            pltpu.VMEM((chunks, 2, tall, columns), f32),
            pltpu.VMEM((2, rows, columns), f32),
            pltpu.VMEM((2, 2, 2, columns, columns), f32),
            pltpu.VMEM((2, 4 * columns, 2 * columns), jnp.bfloat16),
            pltpu.VMEM((2, 4 * columns, 2 * columns), jnp.bfloat16),
            dma((5,)),
            dma((2, steps, chunks)),
            dma((2, steps, chunks)),
            dma((chunks,)),
            dma((chunks,)),
            dma((chunks,)),
            dma((chunks,)),
            dma((2, steps, chunks)),
            dma((2, steps, chunks)),
        ],
        compiler_params=pltpu.CompilerParams(
            collective_id=0, has_side_effects=True, vmem_limit_bytes=60 * 2**20
        ),
    )(picks, row_order, state[:, 0, 0], gate_one, gate_two)
    live_counts = lax.dynamic_slice_in_dim(counts[0], lax.axis_index("leaf") * block, block)
    keep_mask = jnp.arange(columns, dtype=jnp.int32)[None, :] < live_counts[:, None]
    return jnp.where(keep_mask[None], picked, jnp.zeros_like(picked))[:, None]


def solution(mesh):
    return jax.shard_map(
        shards,
        mesh=mesh,
        in_specs=(
            P(None, "leaf", "bits", None, None),
            P(),
            P(),
            P(),
            P("bits", None),
            P("bits", None),
        ),
        out_specs=P(None, "bits", "leaf", None),
        check_vma=False,
    )
```

time: 552 us -> 288 us (0.52); the launches traced: 543 us -> 288 us
  Pallas kernels: 0 us -> 283 us
  waiting for transfers between devices: 249 us -> 0 us
  local copies, waits for them, and re-layouts: 178 us -> 0.72 us
  matrix products: 63.4 us -> 0 us
  other arithmetic: 35.7 us -> 3.32 us
  between operations: 14 us -> 0.02 us
    pallas_call x0 -> x1, Pallas kernels: none -> 283 us  [shards(): pl.pallas_call(functools.partial(kernel, n_leaf), out_shape=jax.ShapeDtyp...]
    reduce_scatter x1 -> x0, waiting for transfers between devices: 145 us -> none  [shards(): lax.psum_scatter(amplitude, 'leaf', scatter_dimension=1, tiled=True)]
    ppermute x2 -> x0, waiting for transfers between devices: 103 us -> none  [from_partner(): lax.ppermute(x, axis, [(i, i ^ 1 << apart) for i in range(lax.axis_size(a...]
    gather x3 -> x0, local copies, waits for them, and re-layouts: 98 us -> none  [the longest x1 37.5 us: shards(): other_rows = jnp.take(partner_two, wanted, axis=1)]
    dot_general x4 -> x0, matrix products: 63.4 us -> none  [complex_product(): jnp.dot(stacked, blocked, precision=lax.Precision.HIGHEST, preferred_elem...]
    ppermute x1 -> x0, local copies, waits for them, and re-layouts: 26.3 us -> none  [from_partner(): lax.ppermute(x, axis, [(i, i ^ 1 << apart) for i in range(lax.axis_size(a...]
    select_n x2 -> x0, other arithmetic: 16.9 us -> none  [the longest x1 16.9 us: shards(): other_rows = jnp.take(partner_two, wanted, axis=1)]
    add x1 -> x0, local copies, waits for them, and re-layouts: 15.4 us -> none  [shards(): own_term + complex_product(partner, quarter(gate_one, 1 - high_one, high_...]
  transfers between devices with their start and end apart: 3 -> 0, of which waited for: 2 -> 0; matrix products, arithmetic and copies ran while one was open for 19% -> 0% of each run, Pallas kernels for 0% -> 0%
where the time goes in v1:
time: 288 us
  Pallas kernels  283 us (98%)
  other arithmetic  3.32 us (1%)
    pallas_call x1, Pallas kernels, shards(): pl.pallas_call(functools.partial(kernel, n_leaf), out_shape=jax.ShapeDtyp...  283 us

profile of v1, /device:TPU:0, one launch (start us, length us, event | category | flops | bytes accessed | tf_op | source)
XLA Modules:
  0.0 287.5 jit_solution(4686562335417971051)
XLA Ops:
  0.0 0.0 copy-start
  0.0 0.7 copy-done
  0.7 0.2 iota_compare_fusion
  0.9 283.5 %shard_map.64 = f32[2,1024,256]{2,1,0:T(8,128)} custom-call(s32[1,4096]{1,0:T(1,128)} %picks_ref.1, s32[4096]{0:T(1024)} %order_ref.1, f32[2,4096,256]{2,1,0:T(8,128)} %bitcast.6, f32[2,512,512]{2,1,0:T(8,128)} %one_ref.1, f32[2,512,512]{2,1,0:T(8,128)} %two_ref.1), custom_call_target="tpu_custom_call" | custom-call | tf_op jit(solution)/shard_map/pallas_call | solution.py:260
  284.4 3.1 %select_bitcast_fusion = f32[2,1,1024,256]{3,2,1,0:T(8,128)} fusion(f32[2,1024,256]{2,1,0:T(8,128)} %shard_map.64, pred[1024,256]{1,0:T(8,128)(4,1)S(1)} %iota_compare_fusion), kind=kLoop, calls=%fused_computation | loop fusion | flops 524288 | bytes 4456448 | tf_op jit(solution)/shard_map/broadcast_in_dim | solution.py:292
  (1 shorter events, 0.0 us)
Async XLA Ops:
  0.0 0.7 copy-start

commit v2 on v1

v2 whole, which is shorter than its diff:
```python
import functools

import jax
import jax.numpy as jnp
from jax import lax
from jax.experimental import pallas as pl
from jax.experimental.pallas import tpu as pltpu
from jax.sharding import PartitionSpec as P

SWAP_ONE = 0
SWAP_TWO = 2
CHUNKS = 8
MESH = pl.DeviceIdType.MESH


def split(x):
    hi = x.astype(jnp.bfloat16)
    lo = (x - hi.astype(jnp.float32)).astype(jnp.bfloat16)
    return hi, lo


def kernel(
    n_leaf, picks_ref, order_ref, state_ref, one_ref, two_ref, out_ref,
    st, rs, ssum, core, sec, ybuf, parts, quarters, w_hi, w_lo,
    local_sem, rs_send, rs_recv, core_send, core_recv, y_send, y_recv, ag_send, ag_recv,
):
    me = lax.axis_index("leaf")
    group = lax.axis_index("bits")
    columns = state_ref.shape[2]
    block = state_ref.shape[1] // n_leaf
    tall = block // CHUNKS
    final = n_leaf - 1
    inner = (me > 0) & (me < final)
    high_one = group // 2**SWAP_ONE % 2
    high_two = group // 2**SWAP_TWO % 2
    partner_one = group + 2**SWAP_ONE * (1 - 2 * high_one)
    partner_two = group + 2**SWAP_TWO * (1 - 2 * high_two)
    neighbour = [lax.rem(me + 1, n_leaf), lax.rem(me + n_leaf - 1, n_leaf)]
    has = [me < final, me > 0]

    barrier = pltpu.get_barrier_semaphore()
    for d in range(2):

        @pl.when(has[d])
        def _():
            pl.semaphore_signal(
                barrier, inc=1, device_id={"leaf": neighbour[d]}, device_id_type=MESH
            )

    for partner in (partner_one, partner_two):
        pl.semaphore_signal(barrier, inc=1, device_id={"bits": partner}, device_id_type=MESH)
    load = pltpu.make_async_copy(state_ref, st, local_sem.at[0])
    load.start()
    loads = []
    for gate, ref, high in ((0, one_ref, high_one), (1, two_ref, high_two)):
        for other in range(2):
            row_half = high if other == 0 else 1 - high
            loads.append(
                pltpu.make_async_copy(
                    ref.at[:, pl.ds(pl.multiple_of(row_half * columns, columns), columns),
                           pl.ds(pl.multiple_of(high * columns, columns), columns)],
                    quarters.at[gate, other],
                    local_sem.at[1 + 2 * gate + other],
                )
            )
            loads[-1].start()

    @pl.when(inner)
    def _():
        pl.semaphore_wait(barrier, 4)

    @pl.when(jnp.logical_not(inner))
    def _():
        pl.semaphore_wait(barrier, 3)


    def rows_of(j, c):
        return pl.ds(pl.multiple_of(j * block + c * tall, tall), tall)

    def rs_copy(d, j, c, src=None):
        return pltpu.make_async_remote_copy(
            src_ref=rs.at[d, j, c] if src is None else src, dst_ref=rs.at[d, j, c],
            send_sem=rs_send.at[d, j, c], recv_sem=rs_recv.at[d, j, c],
            device_id={"leaf": neighbour[d]}, device_id_type=MESH,
        )

    def core_copy(c):
        return pltpu.make_async_remote_copy(
            src_ref=ssum.at[c], dst_ref=core.at[c],
            send_sem=core_send.at[c], recv_sem=core_recv.at[c],
            device_id={"bits": partner_one}, device_id_type=MESH,
        )

    def y_copy(c):
        return pltpu.make_async_remote_copy(
            src_ref=sec.at[c], dst_ref=ybuf.at[c],
            send_sem=y_send.at[c], recv_sem=y_recv.at[c],
            device_id={"bits": partner_two}, device_id_type=MESH,
        )

    def ag_copy(d, j, c):
        piece = parts.at[:, rows_of(j, c), :]
        return pltpu.make_async_remote_copy(
            src_ref=piece, dst_ref=piece,
            send_sem=ag_send.at[d, j, c], recv_sem=ag_recv.at[d, j, c],
            device_id={"leaf": neighbour[d]}, device_id_type=MESH,
        )

    def each(count, body):
        def step(i, carry):
            body(i)
            return carry

        lax.fori_loop(0, count, step, 0)

    def product(gate, mine, theirs):
        x = jnp.concatenate([mine[0], mine[1], theirs[0], theirs[1]], axis=1)
        x_hi, x_lo = split(x)
        dot = functools.partial(jnp.dot, preferred_element_type=jnp.float32)
        return dot(x_hi, w_hi[gate]) + (dot(x_lo, w_hi[gate]) + dot(x_hi, w_lo[gate]))

    @pl.when(me == 0)
    def _():
        def begin(i):
            c, j = i // final, final - i % final
            rs_copy(0, j, c, state_ref.at[:, rows_of(j, c), :]).start()

        each(CHUNKS * final, begin)

    @pl.when(me == final)
    def _():
        def begin(i):
            c, j = i // final, i % final
            rs_copy(1, j, c, state_ref.at[:, rows_of(j, c), :]).start()

        each(CHUNKS * final, begin)

    for one in loads:
        one.wait()
    for gate in range(2):
        for other in range(2):
            re_hi, re_lo = split(quarters[gate, other, 0])
            im_hi, im_lo = split(quarters[gate, other, 1])
            top = pl.ds(2 * other * columns, columns)
            low = pl.ds((2 * other + 1) * columns, columns)
            left, right = pl.ds(0, columns), pl.ds(columns, columns)
            for w, re, im in ((w_hi, re_hi, im_hi), (w_lo, re_lo, im_lo)):
                w[gate, top, left] = re
                w[gate, top, right] = im
                w[gate, low, left] = -im
                w[gate, low, right] = re
    load.wait()

    def reduce_on(c):
        def toward(k):
            for d, j, ahead in ((0, final - k, final - k > me), (1, k, k < me)):

                @pl.when(inner & ahead)
                def _():
                    rs_copy(d, j, c).wait_recv()
                    rs[d, j, c] = rs[d, j, c] + st[:, rows_of(j, c), :]
                    rs_copy(d, j, c).start()

        each(final, toward)

    def gather_near(c):
        for d, j, there in (
            (0, me - 1, (me < final) & (me > 1)), (1, me + 1, (me > 0) & (me < final - 1))
        ):

            @pl.when(there)
            def _():
                ag_copy(d, j, c).wait_recv()
                ag_copy(d, j, c).start()

    def second_step(c):
        y_copy(c).wait_recv()
        part = product(1, sec[c], ybuf[c])
        here = rows_of(me, c)
        parts[0, here, :] = part[:, :columns]
        parts[1, here, :] = part[:, columns:]
        for d in range(2):

            @pl.when(has[d])
            def _():
                ag_copy(d, me, c).start()

    def own_sum(c):
        @pl.when(me > 0)
        def _():
            rs_copy(0, me, c).wait_recv()

        @pl.when(me < final)
        def _():
            rs_copy(1, me, c).wait_recv()

        mine = rows_of(me, c)

        @pl.when(me == 0)
        def _():
            ssum[c] = st[:, mine, :] + rs[1, me, c]

        @pl.when(me == final)
        def _():
            ssum[c] = st[:, mine, :] + rs[0, me, c]

        @pl.when(inner)
        def _():
            ssum[c] = st[:, mine, :] + rs[0, me, c] + rs[1, me, c]

        core_copy(c).start()

    def first_step(c):
        core_copy(c).wait_recv()
        section = product(0, ssum[c], core[c])
        sec[c, 0] = section[:, :columns]
        sec[c, 1] = section[:, columns:]
        y_copy(c).start()

    def iteration(g):
        @pl.when(g < CHUNKS)
        def _():
            reduce_on(g)
            own_sum(g)

        @pl.when(g >= 2)
        def _():
            gather_near(g - 2)

        @pl.when(g < CHUNKS)
        def _():
            first_step(g)

        @pl.when((g >= 1) & (g < CHUNKS + 1))
        def _():
            second_step(g - 1)

    each(CHUNKS + 2, iteration)

    def gather_rest(i):
        c, k = i // n_leaf, i % n_leaf
        late = (k < me) & ((k < me - 1) | (k == 0) | (me == final))

        @pl.when(late)
        def _():
            ag_copy(0, k, c).wait_recv()

            @pl.when(me < final)
            def _():
                ag_copy(0, k, c).start()

        late_right = (k > me) & ((k > me + 1) | (k == final) | (me == 0))

        @pl.when(late_right)
        def _():
            ag_copy(1, k, c).wait_recv()

            @pl.when(me > 0)
            def _():
                ag_copy(1, k, c).start()

    each(CHUNKS * n_leaf, gather_rest)

    base = me * block
    unroll = 16

    def pick(i):
        for k in range(unroll):
            p = i * unroll + k
            row = order_ref[picks_ref[0, base + p]]
            out_ref[:, pl.ds(p, 1), :] = parts[:, pl.ds(row, 1), :]

    each(block // unroll, pick)

    def drain(i):
        c, j = i // n_leaf, i % n_leaf
        for d, sent, gathered in ((0, j > me, j <= me), (1, j < me, j >= me)):

            @pl.when(has[d] & sent)
            def _():
                rs_copy(d, j, c).wait_send()

            @pl.when(has[d] & gathered)
            def _():
                ag_copy(d, j, c).wait_send()

        @pl.when(j == 0)
        def _():
            core_copy(c).wait_send()
            y_copy(c).wait_send()

    each(CHUNKS * n_leaf, drain)


def shards(state, gate_one, gate_two, row_order, picks, counts):
    rows, columns = state.shape[-2:]
    n_leaf = lax.axis_size("leaf")
    block = rows // n_leaf
    tall = block // CHUNKS
    f32, dma = jnp.float32, pltpu.SemaphoreType.DMA
    vmem, smem, hbm = (
        pl.BlockSpec(memory_space=m) for m in (pltpu.VMEM, pltpu.SMEM, pl.ANY)
    )
    picked = pl.pallas_call(
        functools.partial(kernel, n_leaf),
        out_shape=jax.ShapeDtypeStruct((2, block, columns), f32),
        in_specs=[smem, smem, hbm, hbm, hbm],
        out_specs=vmem,
        scratch_shapes=[
            pltpu.VMEM((2, rows, columns), f32),
            pltpu.VMEM((2, n_leaf, CHUNKS, 2, tall, columns), f32),
            pltpu.VMEM((CHUNKS, 2, tall, columns), f32),
            pltpu.VMEM((CHUNKS, 2, tall, columns), f32),
            pltpu.VMEM((CHUNKS, 2, tall, columns), f32),
            pltpu.VMEM((CHUNKS, 2, tall, columns), f32),
            pltpu.VMEM((2, rows, columns), f32),
            pltpu.VMEM((2, 2, 2, columns, columns), f32),
            pltpu.VMEM((2, 4 * columns, 2 * columns), jnp.bfloat16),
            pltpu.VMEM((2, 4 * columns, 2 * columns), jnp.bfloat16),
            dma((5,)),
            dma((2, n_leaf, CHUNKS)),
            dma((2, n_leaf, CHUNKS)),
            dma((CHUNKS,)),
            dma((CHUNKS,)),
            dma((CHUNKS,)),
            dma((CHUNKS,)),
            dma((2, n_leaf, CHUNKS)),
            dma((2, n_leaf, CHUNKS)),
        ],
        compiler_params=pltpu.CompilerParams(
            collective_id=0, has_side_effects=True, vmem_limit_bytes=60 * 2**20
        ),
    )(picks, row_order, state[:, 0, 0], gate_one, gate_two)
    live_counts = lax.dynamic_slice_in_dim(counts[0], lax.axis_index("leaf") * block, block)
    keep_mask = jnp.arange(columns, dtype=jnp.int32)[None, :] < live_counts[:, None]
    return jnp.where(keep_mask[None], picked, jnp.zeros_like(picked))[:, None]


def solution(mesh):
    return jax.shard_map(
        shards,
        mesh=mesh,
        in_specs=(
            P(None, "leaf", "bits", None, None),
            P(),
            P(),
            P(),
            P("bits", None),
            P("bits", None),
        ),
        out_specs=P(None, "bits", "leaf", None),
        check_vma=False,
    )
```

time: 288 us -> 363 us (1.26)
  Pallas kernels: 283 us -> 358 us
    pallas_call x1, Pallas kernels: 283 us -> 358 us  [shards(): pl.pallas_call(functools.partial(kernel, n_leaf), out_shape=jax.ShapeDtyp...]
where the time goes in v2:
time: 363 us; the launch traced here: 362 us
  Pallas kernels  358 us (99%)
    pallas_call x1, Pallas kernels, shards(): pl.pallas_call(functools.partial(kernel, n_leaf), out_shape=jax.ShapeDtyp...  358 us

profile of v2, /device:TPU:0, one launch (start us, length us, event | category | flops | bytes accessed | tf_op | source)
XLA Modules:
  0.0 362.1 jit_solution(13183363920629720588)
XLA Ops:
  0.0 0.0 copy-start
  0.0 0.7 copy-done
  0.7 0.2 iota_compare_fusion
  0.9 358.0 %shard_map.64 = f32[2,1024,256]{2,1,0:T(8,128)} custom-call(s32[1,4096]{1,0:T(1,128)} %picks_ref.1, s32[4096]{0:T(1024)} %order_ref.1, f32[2,4096,256]{2,1,0:T(8,128)} %bitcast.6, f32[2,512,512]{2,1,0:T(8,128)} %one_ref.1, f32[2,512,512]{2,1,0:T(8,128)} %two_ref.1), custom_call_target="tpu_custom_call" | custom-call | tf_op jit(solution)/shard_map/pallas_call | solution.py:304
  359.0 3.1 select_bitcast_fusion
  (1 shorter events, 0.0 us)
Async XLA Ops:
  0.0 0.7 copy-start

commit v3 on v2

--- a/solution.py
+++ b/solution.py
@@ -9,7 +9,7 @@
 
 SWAP_ONE = 0
 SWAP_TWO = 2
-CHUNKS = 8
+CHUNKS = 16
 MESH = pl.DeviceIdType.MESH
 
 
@@ -30,6 +30,7 @@
     block = state_ref.shape[1] // n_leaf
     tall = block // CHUNKS
     final = n_leaf - 1
+    hold = max(CHUNKS - final - 4, 0)
     inner = (me > 0) & (me < final)
     high_one = group // 2**SWAP_ONE % 2
     high_two = group // 2**SWAP_TWO % 2
@@ -119,21 +120,19 @@
         dot = functools.partial(jnp.dot, preferred_element_type=jnp.float32)
         return dot(x_hi, w_hi[gate]) + (dot(x_lo, w_hi[gate]) + dot(x_hi, w_lo[gate]))
 
-    @pl.when(me == 0)
-    def _():
-        def begin(i):
-            c, j = i // final, final - i % final
-            rs_copy(0, j, c, state_ref.at[:, rows_of(j, c), :]).start()
-
-        each(CHUNKS * final, begin)
-
-    @pl.when(me == final)
-    def _():
-        def begin(i):
-            c, j = i // final, i % final
-            rs_copy(1, j, c, state_ref.at[:, rows_of(j, c), :]).start()
-
-        each(CHUNKS * final, begin)
+    def begin(c):
+        def send(k):
+            @pl.when(me == 0)
+            def _():
+                rs_copy(0, final - k, c, state_ref.at[:, rows_of(final - k, c), :]).start()
+
+            @pl.when(me == final)
+            def _():
+                rs_copy(1, k, c, state_ref.at[:, rows_of(k, c), :]).start()
+
+        each(final, send)
+
+    each(2, begin)
 
     for one in loads:
         one.wait()
@@ -151,15 +150,15 @@
                 w[gate, low, right] = re
     load.wait()
 
-    def reduce_on(c):
+    def reduce_on(d, c):
         def toward(k):
-            for d, j, ahead in ((0, final - k, final - k > me), (1, k, k < me)):
-
-                @pl.when(inner & ahead)
-                def _():
-                    rs_copy(d, j, c).wait_recv()
-                    rs[d, j, c] = rs[d, j, c] + st[:, rows_of(j, c), :]
-                    rs_copy(d, j, c).start()
+            j, ahead = ((final - k, final - k > me), (k, k < me))[d]
+
+            @pl.when(ahead)
+            def _():
+                rs_copy(d, j, c).wait_recv()
+                rs[d, j, c] = rs[d, j, c] + st[:, rows_of(j, c), :]
+                rs_copy(d, j, c).start()
 
         each(final, toward)
 
@@ -172,6 +171,13 @@
             def _():
                 ag_copy(d, j, c).wait_recv()
                 ag_copy(d, j, c).start()
+
+    def gather_own(c):
+        for d in range(2):
+
+            @pl.when(has[d])
+            def _():
+                ag_copy(d, me, c).start()
 
     def second_step(c):
         y_copy(c).wait_recv()
@@ -179,11 +185,14 @@
         here = rows_of(me, c)
         parts[0, here, :] = part[:, :columns]
         parts[1, here, :] = part[:, columns:]
-        for d in range(2):
-
-            @pl.when(has[d])
-            def _():
-                ag_copy(d, me, c).start()
+
+        @pl.when(inner | (c >= hold))
+        def _():
+            gather_own(c)
+
+        @pl.when(jnp.logical_not(inner) & (c == hold))
+        def _():
+            each(hold, gather_own)
 
     def own_sum(c):
         @pl.when(me > 0)
@@ -217,25 +226,36 @@
         sec[c, 1] = section[:, columns:]
         y_copy(c).start()
 
-    def iteration(g):
-        @pl.when(g < CHUNKS)
-        def _():
-            reduce_on(g)
+    def iteration(i):
+        g = i - final
+
+        @pl.when(i + 2 < CHUNKS)
+        def _():
+            begin(i + 2)
+
+        @pl.when((g >= 0) & (g < CHUNKS))
+        def _():
             own_sum(g)
 
-        @pl.when(g >= 2)
-        def _():
-            gather_near(g - 2)
-
-        @pl.when(g < CHUNKS)
+        for d, c in ((0, g + final - me), (1, g + me)):
+
+            @pl.when(inner & (c >= 0) & (c < CHUNKS))
+            def _():
+                reduce_on(d, c)
+
+        @pl.when(g >= 3)
+        def _():
+            gather_near(g - 3)
+
+        @pl.when((g >= 1) & (g < CHUNKS + 1))
+        def _():
+            second_step(g - 1)
+
+        @pl.when((g >= 0) & (g < CHUNKS))
         def _():
             first_step(g)
 
-        @pl.when((g >= 1) & (g < CHUNKS + 1))
-        def _():
-            second_step(g - 1)
-
-    each(CHUNKS + 2, iteration)
+    each(final + CHUNKS + 3, iteration)
 
     def gather_rest(i):
         c, k = i // n_leaf, i % n_leaf

time: 363 us -> 317 us (0.87)
  Pallas kernels: 358 us -> 313 us
    pallas_call x1, Pallas kernels: 358 us -> 313 us  [shards(): pl.pallas_call(functools.partial(kernel, n_leaf), out_shape=jax.ShapeDtyp...]
where the time goes in v3:
time: 317 us
  Pallas kernels  313 us (99%)
  other arithmetic  3.32 us (1%)
    pallas_call x1, Pallas kernels, shards(): pl.pallas_call(functools.partial(kernel, n_leaf), out_shape=jax.ShapeDtyp...  313 us

profile of v3, /device:TPU:0, one launch (start us, length us, event | category | flops | bytes accessed | tf_op | source)
XLA Modules:
  0.0 316.6 jit_solution(8255021251051760148)
XLA Ops:
  0.0 0.0 copy-start
  0.0 0.7 copy-done
  0.7 0.2 iota_compare_fusion
  0.9 312.5 %shard_map.64 = f32[2,1024,256]{2,1,0:T(8,128)} custom-call(s32[1,4096]{1,0:T(1,128)} %picks_ref.1, s32[4096]{0:T(1024)} %order_ref.1, f32[2,4096,256]{2,1,0:T(8,128)} %bitcast.6, f32[2,512,512]{2,1,0:T(8,128)} %one_ref.1, f32[2,512,512]{2,1,0:T(8,128)} %two_ref.1), custom_call_target="tpu_custom_call" | custom-call | tf_op jit(solution)/shard_map/pallas_call | solution.py:324
  313.5 3.1 select_bitcast_fusion
  (1 shorter events, 0.0 us)
Async XLA Ops:
  0.0 0.7 copy-start

commit v4 on v3

--- a/solution.py
+++ b/solution.py
@@ -30,7 +30,7 @@
     block = state_ref.shape[1] // n_leaf
     tall = block // CHUNKS
     final = n_leaf - 1
-    hold = max(CHUNKS - final - 4, 0)
+    hold = max(CHUNKS - final - 5, 0)
     inner = (me > 0) & (me < final)
     high_one = group // 2**SWAP_ONE % 2
     high_two = group // 2**SWAP_TWO % 2
@@ -243,19 +243,19 @@
             def _():
                 reduce_on(d, c)
 
-        @pl.when(g >= 3)
-        def _():
-            gather_near(g - 3)
-
-        @pl.when((g >= 1) & (g < CHUNKS + 1))
-        def _():
-            second_step(g - 1)
+        @pl.when(g >= 4)
+        def _():
+            gather_near(g - 4)
+
+        @pl.when((g >= 2) & (g < CHUNKS + 2))
+        def _():
+            second_step(g - 2)
 
         @pl.when((g >= 0) & (g < CHUNKS))
         def _():
             first_step(g)
 
-    each(final + CHUNKS + 3, iteration)
+    each(final + CHUNKS + 4, iteration)
 
     def gather_rest(i):
         c, k = i // n_leaf, i % n_leaf

time: 317 us -> 315 us (level)
  no operation moved by 1% of the time
where the time goes in v4:
time: 315 us; the launch traced here: 314 us
  Pallas kernels  310 us (98%)
  other arithmetic  3.32 us (1%)
    pallas_call x1, Pallas kernels, shards(): pl.pallas_call(functools.partial(kernel, n_leaf), out_shape=jax.ShapeDtyp...  310 us

profile of v4, /device:TPU:0, one launch (start us, length us, event | category | flops | bytes accessed | tf_op | source)
XLA Modules:
  0.0 314.4 jit_solution(13532907772613958019)
XLA Ops:
  0.0 0.0 copy-start
  0.0 0.7 copy-done
  0.7 0.2 iota_compare_fusion
  0.9 310.3 %shard_map.64 = f32[2,1024,256]{2,1,0:T(8,128)} custom-call(s32[1,4096]{1,0:T(1,128)} %picks_ref.1, s32[4096]{0:T(1024)} %order_ref.1, f32[2,4096,256]{2,1,0:T(8,128)} %bitcast.6, f32[2,512,512]{2,1,0:T(8,128)} %one_ref.1, f32[2,512,512]{2,1,0:T(8,128)} %two_ref.1), custom_call_target="tpu_custom_call" | custom-call | tf_op jit(solution)/shard_map/pallas_call | solution.py:324
  311.3 3.1 select_bitcast_fusion
  (1 shorter events, 0.0 us)
Async XLA Ops:
  0.0 0.7 copy-start
